TPU v7x, 32 devices: a whole 2x2x4 slice. The times are simulated.
32 devices in a mesh: dp: 32 (over z, y, x, core).
Axes of the slice: x: 2, y: 2, z: 4, core: 2. Of those that a mesh axis runs over, the one named last changes fastest.
Arguments:
- text_states: bfloat16 [512, 16, 768], P('dp'), may hold values from -6 to 6
- text_len: int32 [512], P('dp'), may hold values from 1 to 16
- query_states: bfloat16 [512, 16, 768], P('dp'), may hold values from -6 to 6
- neg_owner: int32 [512, 2], P('dp'), may hold values from 0 to 31, all different within a row; in each aligned block of 16 rows (0 to 15, 16 to 31, ...) at most 2 rows name the same one
- neg_slot: int32 [512, 2], P('dp'), may hold values from 0 to 15
- projection_weight: bfloat16 [768, 2304], replicated, may hold values from -0.21875 to 0.21875
- output_weight: bfloat16 [768, 768], replicated, may hold values from -0.21875 to 0.21875
- ln_gain: float32 [768], replicated, may hold values from 0.5 to 1.5
- ln_bias: float32 [768], replicated, may hold values from -3 to 3
- itm_weight: float32 [768, 2], replicated, may hold values from -0.875 to 0.875
- itm_bias: float32 [2], replicated, may hold values from -3 to 3
Outputs:
- pair_logits: float32 [512, 3, 2], P('dp')
- grad_text: bfloat16 [512, 16, 768], P('dp')
- grad_query: bfloat16 [512, 16, 768], P('dp')
- grad_qkv: float32 [768, 2304], replicated
- grad_out: float32 [768, 768], replicated
Inputs may be any that keep to these rules, and one draw needn't show every extreme that they name: `neg_owner`: the two negatives of a caption lie in different blocks; among the 16 captions of one device no block is named more than 2 times, and in some device exactly 2 times.
All inputs are finite; a program needn't handle non-finite values.
Results may differ from a plain program's by a relative error of at most 0.0075.
Values may be sent and summed in bfloat16 or wider, within the bound.
No kernel may reach another device: no remote copies, remote signals or barrier semaphores. Data moves between devices by JAX's collectives and lax.ppermute only.
A program may use at most 128 MiB of HBM per device.

v0:
```python
import math

import jax
import jax.numpy as jnp
from jax import lax
from jax.sharding import PartitionSpec as P

HEADS = 12
CAP = 2


def matrix_product(einsum_form, left_side, right_side):
    return jnp.einsum(einsum_form, left_side, right_side, preferred_element_type=jnp.float32)


def split_heads(tensor, head_number):
    return tensor.reshape(tensor.shape[:-1] + (head_number, tensor.shape[-1] // head_number))


def merge_heads(tensor):
    return tensor.reshape(tensor.shape[0], tensor.shape[1], tensor.shape[2] * tensor.shape[3])


def tail_loss(hidden_states, ln_gain, ln_bias, itm_weight, itm_bias, labels):
    center = hidden_states - jnp.mean(hidden_states, axis=-1, keepdims=True)
    spread = jnp.mean(center * center, axis=-1, keepdims=True)
    normed = center * lax.rsqrt(spread + 1e-06) * ln_gain + ln_bias
    pooled = jnp.mean(normed, axis=1)
    logits = jnp.dot(pooled, itm_weight, precision=lax.Precision.HIGHEST) + itm_bias
    losses = jax.nn.logsumexp(logits, axis=-1) - jnp.sum(logits * labels, axis=-1)
    return (jnp.sum(losses), logits)


def pair_work(
    caption_rows,
    lengths,
    images,
    projection_weight,
    output_weight,
    ln_gain,
    ln_bias,
    itm_weight,
    itm_bias,
):
    caption_texts, text_rows, hidden_width = caption_rows.shape
    query_row_count = images.shape[2]
    pair_rows = caption_texts * 3
    head_number = HEADS
    score_scale = 1.0 / math.sqrt(hidden_width // head_number)
    text_kv = matrix_product(
        "bld,de->ble", caption_rows, projection_weight[:, hidden_width:]
    ).astype(jnp.bfloat16)
    image_row_count = images.reshape(pair_rows, query_row_count, hidden_width)
    image_projected = matrix_product("tns,sm->tnm", image_row_count, projection_weight).astype(
        jnp.bfloat16
    )
    text_wide = jnp.broadcast_to(
        text_kv[:, None], (caption_texts, 3, text_rows, 2 * hidden_width)
    ).reshape(pair_rows, text_rows, 2 * hidden_width)
    queries = split_heads(image_projected[:, :, :hidden_width], head_number)
    key_heads = split_heads(
        jnp.concatenate(
            [
                image_projected[:, :, hidden_width : 2 * hidden_width],
                text_wide[:, :, :hidden_width],
            ],
            axis=1,
        ),
        head_number,
    )
    value_heads = split_heads(
        jnp.concatenate(
            [image_projected[:, :, 2 * hidden_width :], text_wide[:, :, hidden_width:]], axis=1
        ),
        head_number,
    )
    position = jnp.arange(query_row_count + text_rows)
    key_valid = (position[None, :] < query_row_count) | (
        position[None, :] - query_row_count < lengths[:, None]
    )
    key_valid = jnp.repeat(key_valid, 3, axis=0)
    scores = matrix_product("bqhe,bkhe->bhqk", queries, key_heads) * score_scale
    scores = jnp.where(key_valid[:, None, None, :], scores, -1e30)
    shifted = jnp.exp(scores - jnp.max(scores, axis=-1, keepdims=True))
    weights = shifted / jnp.sum(shifted, axis=-1, keepdims=True)
    weights_low = weights.astype(jnp.bfloat16)
    attended_context = merge_heads(
        matrix_product("bhqk,bkhe->bqhe", weights_low, value_heads).astype(jnp.bfloat16)
    )
    hidden_states = image_row_count.astype(jnp.float32) + matrix_product(
        "tns,sm->tnm", attended_context, output_weight
    )
    labels = jnp.tile(
        jnp.array([[0.0, 1.0], [1.0, 0.0], [1.0, 0.0]], dtype=jnp.float32), (caption_texts, 1)
    )

    def loss_of(hidden_in):
        return tail_loss(hidden_in, ln_gain, ln_bias, itm_weight, itm_bias, labels)

    loss_total, pullback, logits = jax.vjp(loss_of, hidden_states, has_aux=True)
    hidden_gradient = pullback(jnp.ones_like(loss_total))[0]
    attention_gradient = hidden_gradient.astype(jnp.bfloat16)
    output_weight_gradient = matrix_product("nxv,nxl->vl", attended_context, attention_gradient)
    return (
        logits,
        attended_context,
        attention_gradient,
        hidden_gradient,
        output_weight_gradient,
        image_row_count,
        queries,
        key_heads,
        value_heads,
        weights,
        weights_low,
    )


def pair_backward(
    caption_rows,
    projection_weight,
    output_weight,
    query_row_count,
    attention_gradient,
    hidden_gradient,
    queries,
    key_heads,
    value_heads,
    weights,
    weights_low,
):
    caption_texts, text_rows, hidden_width = caption_rows.shape
    head_number = HEADS
    score_scale = 1.0 / math.sqrt(hidden_width // head_number)
    context_gradient = split_heads(
        matrix_product("kvp,mp->kvm", attention_gradient, output_weight).astype(jnp.bfloat16),
        head_number,
    )
    grad_probs = matrix_product("bqhe,bkhe->bhqk", context_gradient, value_heads)
    grad_values = matrix_product("bhqk,bqhe->bkhe", weights_low, context_gradient)
    grad_scores = (
        weights * (grad_probs - jnp.sum(grad_probs * weights, axis=-1, keepdims=True)) * score_scale
    ).astype(jnp.bfloat16)
    grad_queries = merge_heads(matrix_product("bhqk,bkhe->bqhe", grad_scores, key_heads))
    grad_keys = merge_heads(matrix_product("bhqk,bqhe->bkhe", grad_scores, queries))
    grad_values = merge_heads(grad_values)
    image_projection_gradient = jnp.concatenate(
        [grad_queries, grad_keys[:, :query_row_count], grad_values[:, :query_row_count]], axis=-1
    ).astype(jnp.bfloat16)
    grad_text_kv = jnp.concatenate(
        [grad_keys[:, query_row_count:], grad_values[:, query_row_count:]], axis=-1
    )
    grad_text_kv = jnp.sum(
        grad_text_kv.reshape(caption_texts, 3, text_rows, 2 * hidden_width), axis=1
    ).astype(jnp.bfloat16)
    image_gradient = (
        matrix_product("kvp,mp->kvm", image_projection_gradient, projection_weight)
        + hidden_gradient
    ).reshape(caption_texts, 3, query_row_count, hidden_width)
    grad_text = matrix_product("ble,de->bld", grad_text_kv, projection_weight[:, hidden_width:])
    return (grad_text, image_gradient, image_projection_gradient, grad_text_kv)


def on_device(
    text_states,
    text_len,
    query_states,
    neg_owner,
    neg_slot,
    projection_weight,
    output_weight,
    ln_gain,
    ln_bias,
    itm_weight,
    itm_bias,
):
    caption_count = text_states.shape[0]
    query_row_count = query_states.shape[1]
    hidden_width = query_states.shape[2]
    peer_count = lax.axis_size("dp")
    capacity = CAP
    flat_owner = neg_owner.reshape(-1)
    flat_slot = neg_slot.reshape(-1)
    request_count = flat_owner.shape[0]
    request_ids = jnp.arange(request_count)
    same_owner = flat_owner[:, None] == flat_owner[None, :]
    before = request_ids[:, None] > request_ids[None, :]
    rank_within = jnp.sum((same_owner & before).astype(jnp.int32), axis=1)
    bucket = flat_owner * capacity + rank_within
    slot_hot = bucket[:, None] == jnp.arange(peer_count * capacity)[None, :]
    wanted = jnp.sum(jnp.where(slot_hot, flat_slot[:, None] + 1, 0), axis=0).reshape(
        peer_count, capacity
    )
    requested = lax.all_to_all(wanted, "dp", split_axis=0, concat_axis=0, tiled=True)
    send_select = (requested.reshape(-1)[:, None] == jnp.arange(caption_count)[None, :] + 1).astype(
        jnp.bfloat16
    )
    outgoing = jnp.dot(
        send_select, query_states.reshape(caption_count, -1), preferred_element_type=jnp.float32
    ).astype(jnp.bfloat16)
    outgoing = outgoing.reshape(peer_count, capacity, query_row_count, hidden_width)
    fetched = lax.all_to_all(outgoing, "dp", split_axis=0, concat_axis=0, tiled=True)
    take_select = slot_hot.astype(jnp.bfloat16)
    negatives = jnp.dot(
        take_select, fetched.reshape(peer_count * capacity, -1), preferred_element_type=jnp.float32
    ).astype(jnp.bfloat16)
    negatives = negatives.reshape(caption_count, 2, query_row_count, hidden_width)
    images = jnp.concatenate([query_states[:, None], negatives], axis=1)
    (
        logits,
        attended_context,
        attention_gradient,
        hidden_gradient,
        output_weight_gradient,
        image_row_count,
        queries,
        key_heads,
        value_heads,
        weights,
        weights_low,
    ) = pair_work(
        text_states,
        text_len,
        images,
        projection_weight,
        output_weight,
        ln_gain,
        ln_bias,
        itm_weight,
        itm_bias,
    )
    all_pairs = caption_count * peer_count
    grad_text, image_gradient, image_projection_gradient, grad_text_kv = pair_backward(
        text_states,
        projection_weight,
        output_weight,
        query_row_count,
        attention_gradient,
        hidden_gradient,
        queries,
        key_heads,
        value_heads,
        weights,
        weights_low,
    )
    back_rows = image_gradient[:, 1:].astype(jnp.bfloat16).reshape(request_count, -1)
    outgoing_grads = jnp.dot(take_select.T, back_rows, preferred_element_type=jnp.float32).astype(
        jnp.bfloat16
    )
    outgoing_grads = outgoing_grads.reshape(peer_count, capacity, query_row_count, hidden_width)
    returned = lax.all_to_all(outgoing_grads, "dp", split_axis=0, concat_axis=0, tiled=True)
    projection_weight_gradient = matrix_product(
        "nxv,nxl->vl", image_row_count, image_projection_gradient
    )
    projection_weight_gradient = projection_weight_gradient + jnp.pad(
        matrix_product("bld,ble->de", text_states, grad_text_kv), ((0, 0), (hidden_width, 0))
    )
    sum_qkv, sum_out = lax.psum((projection_weight_gradient, output_weight_gradient), "dp")
    received = jnp.dot(
        send_select.T,
        returned.reshape(peer_count * capacity, -1),
        preferred_element_type=jnp.float32,
    )
    grad_query = (
        image_gradient[:, 0] + received.reshape(caption_count, query_row_count, hidden_width)
    ).astype(jnp.bfloat16)
    return (
        logits.reshape(caption_count, 3, 2),
        grad_text.astype(jnp.bfloat16),
        grad_query,
        sum_qkv / all_pairs,
        sum_out / all_pairs,
    )


def solution(mesh):
    placed = (
        P("dp", None, None),
        P("dp"),
        P("dp", None, None),
        P("dp", None),
        P("dp", None),
        P(),
        P(),
        P(),
        P(),
        P(),
        P(),
    )
    return jax.shard_map(
        on_device,
        mesh=mesh,
        in_specs=placed,
        out_specs=(P("dp", None, None), P("dp", None, None), P("dp", None, None), P(), P()),
        check_vma=False,
    )
```

profile of v0, /device:TPU:0, one launch (start us, length us, event | category | flops | bytes accessed | tf_op | source)
XLA Modules:
  0.0 690.8 jit_solution(13503228624553130403)
XLA Ops:
  10.0 7.3 %all-to-all-start = ((s32[32,1,2]{2,1,0:T(1,128)}), s32[32,1,2]{2,1,0:T(1,128)S(1)}, u32[]{:S(2)}, u32[]{:S(2)}) async-start(s32[32,1,2]{2,1,0:T(1,128)} %bitcast.2), calls=%async_computation | async-start | bytes 32768 | tf_op jit(solution)/shard_map/all_to_all | solution.py:194
  18.5 6.0 all-to-all-done
  35.4 33.1 %all-to-all-done.1 = bf16[32,2,16,768]{3,2,1,0:T(8,128)(2,1)S(1)} async-done(((bf16[32,2,16,768]{3,2,1,0:T(8,128)(2,1)}), bf16[32,2,16,768]{3,2,1,0:T(8,128)(2,1)S(1)}, u32[]{:S(2)}, u32[]{:S(2)}) %all-to-all-start.1) | async-done | bytes 1572896 | tf_op jit(solution)/shard_map/all_to_all | solution.py:202
  72.0 3.1 convolution_convert_fusion.3
  78.9 8.2 %reshape.168 = bf16[48,32,12,64]{3,2,1,0:T(8,128)(2,1)} reshape(bf16[48,32,768]{2,1,0:T(8,128)(2,1)} %get-tuple-element.38) | data formatting | bytes 4718592 | tf_op jit(solution)/shard_map/reshape | solution.py:17
  87.0 4.7 reshape.167
  91.7 5.9 reshape.166
  97.6 6.3 fusion.15
  103.9 97.7 %fusion.88 = (f32[48,12,16]{2,1,0:T(8,128)S(1)}, f32[48,12,16,32]{3,2,1,0:T(8,128)S(1)}) fusion(f32[48,12,16,32]{3,2,1,0:T(8,128)S(1)} %fusion.15, pred[48,32]{1,0:T(8,128)(4,1)S(1)} %broadcast_in_dim.85), kind=kOutput, calls=%fused_computation.128 | output fusion | flops 1769503 | bytes 2397696 | tf_op jit(solution)/shard_map/sub | solution.py:84
  206.4 4.9 reshape.169
  217.7 3.0 convolution_bitcast_fusion.3
  223.2 4.7 reshape.171
  227.9 8.6 %fusion.9 = f32[48,12,16,32]{3,2,1,0:T(8,128)} fusion(bf16[48,32,12,64]{3,2,1,0:T(8,128)(2,1)} %reshape.166, bf16[48,16,12,64]{3,2,1,0:T(8,128)(2,1)} %reshape.171), kind=kOutput, calls=%fused_computation.25 | convolution fusion | flops 37748736 | bytes 4718592 | tf_op jit(solution)/shard_map/bqhe,bkhe->bhqk/dot_general | solution.py:13
  236.4 57.6 %convert_bitcast_fusion = bf16[48,16,12,64]{3,1,2,0:T(8,128)(2,1)} fusion(bf16[48,32,12,64]{3,2,1,0:T(8,128)(2,1)} %reshape.168, f32[48,12,16,32]{3,2,1,0:T(8,128)} %fusion.9, f32[48,12,16,32]{3,2,1,0:T(8,128)} %copy-done.41, f32[48,12,16]{2,1,0:T(8,128)S(1)} %copy-done.43), kind=kOutput, calls=%fused_computation.42 | convolution fusion | flops 40412192 | bytes 5935104 | tf_op jit(solution)/shard_map/bhqk,bkhe->bqhe/dot_general | solution.py:13
  294.0 60.9 %convolution_bitcast_fusion.2 = f32[48,32,12,64]{3,1,2,0:T(8,128)} fusion(bf16[48,16,12,64]{3,2,1,0:T(8,128)(2,1)} %reshape.167, f32[48,12,16,32]{3,2,1,0:T(8,128)} %fusion.9, f32[48,12,16,32]{3,2,1,0:T(8,128)} %copy-done.41, f32[48,12,16]{2,1,0:T(8,128)S(1)} %copy-done.43), kind=kOutput, calls=%fused_computation.22 | convolution fusion | flops 39822368 | bytes 8294400 | tf_op jit(solution)/shard_map/bhqk,bqhe->bkhe/dot_general | solution.py:13
  355.0 10.9 %convolution_bitcast_fusion.1 = f32[48,32,12,64]{3,1,2,0:T(8,128)} fusion(bf16[48,16,12,64]{3,2,1,0:T(8,128)(2,1)} %reshape.171, f32[48,12,16,32]{3,2,1,0:T(8,128)} %copy-done.41, f32[48,12,16]{2,1,0:T(8,128)S(1)} %copy-done.43), kind=kOutput, calls=%fused_computation.21 | convolution fusion | flops 38338560 | bytes 7114752 | tf_op jit(solution)/shard_map/bhqk,bqhe->bkhe/dot_general | solution.py:13
  365.8 13.5 %copy.92 = f32[48,32,12,64]{3,2,1,0:T(8,128)} copy(f32[48,32,12,64]{3,1,2,0:T(8,128)S(1)} %copy-done.3) | data formatting | bytes 9437184 | tf_op jit(solution)/shard_map/bhqk,bqhe->bkhe/transpose | solution.py:13
  379.3 9.9 %reshape.172 = f32[48,32,768]{2,1,0:T(8,128)} reshape(f32[48,32,12,64]{3,2,1,0:T(8,128)} %copy.92) | data formatting | bytes 9437184 | tf_op jit(solution)/shard_map/reshape | solution.py:21
  389.2 3.2 slice.57
  395.4 16.9 %copy.94 = f32[48,32,12,64]{3,2,1,0:T(8,128)} copy(f32[48,32,12,64]{3,1,2,0:T(8,128)} %convolution_bitcast_fusion.1) | data formatting | bytes 9437184 | tf_op jit(solution)/shard_map/bhqk,bqhe->bkhe/transpose | solution.py:13
  412.3 10.2 %reshape.173 = f32[48,32,768]{2,1,0:T(8,128)} reshape(f32[48,32,12,64]{3,2,1,0:T(8,128)} %copy.94) | data formatting | bytes 9437184 | tf_op jit(solution)/shard_map/reshape | solution.py:21
  422.5 3.4 slice.58
  431.3 4.8 reshape.175
  436.0 5.2 pad_maximum_fusion
  441.2 3.0 reduce_sum.117
  446.6 5.6 bitcast_add_fusion
  453.1 5.9 add_add_fusion.1
  461.8 3.6 all-to-all-start.2
  467.4 3.3 fusion.49
  470.7 49.5 %all-to-all-done.2 = bf16[32,2,16,768]{3,2,1,0:T(8,128)(2,1)S(1)} async-done(((bf16[32,2,16,768]{3,2,1,0:T(8,128)(2,1)}), bf16[32,2,16,768]{3,2,1,0:T(8,128)(2,1)S(1)}, u32[]{:S(2)}, u32[]{:S(2)}) %all-to-all-start.2) | async-done | bytes 1572896 | tf_op jit(solution)/shard_map/all_to_all | solution.py:251
  522.0 153.2 %all-reduce.4.cloned.1.call-done = (f32[768,2304]{1,0:T(8,128)}, f32[768,768]{1,0:T(8,128)}) async-done(((f32[768,2304]{1,0:T(8,128)}, f32[768,768]{1,0:T(8,128)}), (f32[768,2304]{1,0:T(8,128)}, f32[768,768]{1,0:T(8,128)})) %all-reduce.4.cloned.1.call-update) | async-done | bytes 9437200 | tf_op jit(solution)/shard_map/psum | solution.py:258
  675.2 6.6 broadcast_multiply_fusion
  (154 shorter events, 55.2 us)
Async XLA Ops:
  7.2 204.2 %copy-start = (bf16[768,768]{1,0:T(8,128)(2,1)S(1)}, bf16[768,768]{1,0:T(8,128)(2,1)}, u32[]{:S(2)}) copy-start(bf16[768,768]{1,0:T(8,128)(2,1)} %param.18) | copy-start | bytes 3538948
  8.3 60.8 %copy-start.35 = (s32[32]{0:T(128)}, s32[32]{0:T(128)S(1)}, u32[]{:S(2)}) copy-start(s32[32]{0:T(128)S(1)} %multiply_add_fusion.1) | copy-start | bytes 388
  10.0 14.4 %all-to-all-start = ((s32[32,1,2]{2,1,0:T(1,128)}), s32[32,1,2]{2,1,0:T(1,128)S(1)}, u32[]{:S(2)}, u32[]{:S(2)}) async-start(s32[32,1,2]{2,1,0:T(1,128)} %bitcast.2), calls=%async_computation | async-start | bytes 32768 | tf_op jit(solution)/shard_map/all_to_all | solution.py:194
  17.3 10.6 %copy-start.33 = (s32[16]{0:T(128)}, s32[16]{0:T(128)S(1)}, u32[]{:S(2)}) copy-start(s32[16]{0:T(128)S(1)} %iota_add_fusion.1) | copy-start | bytes 196
  25.7 2.2 copy-start.30
  27.9 2.9 copy-start.39
  27.9 3.1 copy-start.37
  27.9 3.2 copy-start.20
  27.9 40.6 %all-to-all-start.1 = ((bf16[32,2,16,768]{3,2,1,0:T(8,128)(2,1)}), bf16[32,2,16,768]{3,2,1,0:T(8,128)(2,1)S(1)}, u32[]{:S(2)}, u32[]{:S(2)}) async-start(bf16[32,2,16,768]{3,2,1,0:T(8,128)(2,1)} %bitcast.105), calls=%async_computation.1 | async-start | bytes 3145728 | tf_op jit(solution)/shard_map/all_to_all | solution.py:202
  30.8 644.4 %all-reduce.4.cloned.1.call-start = ((), (), s32[]{:S(2)}) async-start(), calls=%async_computation.3 | async-start | bytes 18874368 | tf_op jit(solution)/shard_map/psum | solution.py:258
  69.5 2.5 copy-start.40
  75.1 2.0 copy-start.5
  103.9 97.7 %copy-start.2 = (bf16[48,32,12,64]{3,2,1,0:T(8,128)(2,1)S(1)}, bf16[48,32,12,64]{3,2,1,0:T(8,128)(2,1)}, u32[]{:S(2)}) copy-start(bf16[48,32,12,64]{3,2,1,0:T(8,128)(2,1)} %reshape.166) | copy-start | bytes 7077892
  201.6 2.2 copy-start.41
  201.6 2.3 copy-start.42
  214.2 6.5 copy-start.18
  214.9 5.8 copy-start.22
  216.3 4.4 copy-start.9
  216.8 3.9 copy-start.24
  217.7 3.0 copy-start.28
  227.9 8.6 %copy-start.43 = (f32[48,12,16]{2,1,0:T(8,128)S(1)}, f32[48,12,16]{2,1,0:T(8,128)}, u32[]{:S(2)}) copy-start(f32[48,12,16]{2,1,0:T(8,128)} %copy-done.42) | copy-start | bytes 110596
  354.9 10.9 %copy-start.3 = (f32[48,32,12,64]{3,1,2,0:T(8,128)S(1)}, f32[48,32,12,64]{3,1,2,0:T(8,128)}, u32[]{:S(2)}) copy-start(f32[48,32,12,64]{3,1,2,0:T(8,128)} %convolution_bitcast_fusion.2) | copy-start | bytes 14155780
  422.5 6.2 copy-start.7
  441.2 3.0 copy-start.21
  444.2 1.6 copy-start.13
  444.2 2.0 copy-start.14
  444.2 2.3 copy-start.16
  461.8 58.3 %all-to-all-start.2 = ((bf16[32,2,16,768]{3,2,1,0:T(8,128)(2,1)}), bf16[32,2,16,768]{3,2,1,0:T(8,128)(2,1)S(1)}, u32[]{:S(2)}, u32[]{:S(2)}) async-start(bf16[32,2,16,768]{3,2,1,0:T(8,128)(2,1)} %bitcast.107), calls=%async_computation.2 | async-start | bytes 3145728 | tf_op jit(solution)/shard_map/all_to_all | solution.py:251
  467.4 52.7 %copy-start.31 = (s32[64]{0:T(128)S(1)}, s32[64]{0:T(128)}, u32[]{:S(2)}) copy-start(s32[64]{0:T(128)} %copy-done.30) | copy-start | bytes 772
  467.4 52.7 %copy-start.34 = (s32[16]{0:T(128)S(1)}, s32[16]{0:T(128)}, u32[]{:S(2)}) copy-start(s32[16]{0:T(128)} %copy-done.33) | copy-start | bytes 196
  675.2 6.6 copy-start.6
  681.8 1.7 copy-start.1
  (16 other events, 16.9 us)
Sparse Core Ops, SparseCore 0:
  452.3 222.7 all-reduce.3
where the time goes:
time: 700 us; the launch traced here: 691 us
  waiting for transfers between devices  242 us (35%)
  matrix products  179 us (26%)
  local copies, waits for them, and re-layouts  121 us (17%)
  other arithmetic  120 us (17%)
  between operations  15.2 us (2%)
  starting transfers between devices  13.8 us (2%)
    dot_general x15, matrix products, matrix_product(): jnp.einsum(einsum_form, left_side, right_side, preferred_element_type=jnp...  176 us
    psum x1, waiting for transfers between devices, on_device(): lax.psum((projection_weight_gradient, output_weight_gradient), 'dp')  153 us
    sub x1, other arithmetic, pair_work(): shifted = jnp.exp(scores - jnp.max(scores, axis=-1, keepdims=True))  97.7 us
    all_to_all x1, waiting for transfers between devices, on_device(): lax.all_to_all(outgoing_grads, 'dp', split_axis=0, concat_axis=0, tiled=T...  49.5 us
    all_to_all x1, waiting for transfers between devices, on_device(): lax.all_to_all(outgoing, 'dp', split_axis=0, concat_axis=0, tiled=True)  33.1 us
    transpose x3, local copies, waits for them, and re-layouts, matrix_product(): jnp.einsum(einsum_form, left_side, right_side, preferred_element_type=jnp...  32.9 us
    reshape x4, local copies, waits for them, and re-layouts, merge_heads(): tensor.reshape(tensor.shape[0], tensor.shape[1], tensor.shape[2] * tensor...  29.8 us
    reshape x4, local copies, waits for them, and re-layouts, split_heads(): tensor.reshape(tensor.shape[:-1] + (head_number, tensor.shape[-1] // head...  23.4 us
  transfers between devices with their start and end apart: 4, of which 4 were waited for; matrix products, arithmetic and copies ran while one was open for 3% of the time, Pallas kernels for 0%

commit v1 on v0

v1 whole, which is shorter than its diff:
```python
import functools
import jax
import jax.numpy as jnp
from jax import lax
from jax.experimental import pallas as pl
from jax.experimental.pallas import tpu as pltpu

from jax.sharding import PartitionSpec as P

BF = jnp.bfloat16
F32 = jnp.float32


def dot_nt(a, b):
    return lax.dot_general(a, b, (((1,), (1,)), ((), ())), preferred_element_type=F32)


def dot_nn(a, b):
    return lax.dot_general(a, b, (((1,), (0,)), ((), ())), preferred_element_type=F32)


def core_kernel(lens, x, qkv, tkv, wo, gain, bias, head_w, head_b, text_in, logits, gh, ga, ctx, dqkv, dtext, probs, dctx, *, negatives):
    rows, width = x.shape
    pairs_of_units = rows // 64
    quads = width // 256
    scale = 0.125
    lane = lax.broadcasted_iota(jnp.int32, (128, 128), 1)
    left = lane < 64
    lane32 = lax.broadcasted_iota(jnp.int32, (32, 128), 1)
    row32 = lax.broadcasted_iota(jnp.int32, (32, 128), 0)
    qg = row32 // 16
    uu = lane32 // 64
    key = lane32 % 64
    is_image = key < 32
    image_ok = is_image & ((key // 16) == qg)
    tg = (key - 32) // 16
    tpos = key % 16
    text_ok = jnp.logical_not(is_image) & (tg == (uu if negatives else qg))
    half32 = lane32 < 64
    hm_lane = lax.broadcasted_iota(jnp.int32, (1, 256), 1) // 64
    head_mask = [(hm_lane == h).astype(F32).astype(BF) for h in range(4)]
    zero64 = jnp.zeros((64, 256), BF)

    def head_blocks(t):
        return jnp.concatenate([t * m for m in head_mask], axis=0)

    def text_rows(j, u):
        if negatives:
            return pl.ds(pl.multiple_of(j * 32, 32), 32)
        return pl.ds(pl.multiple_of(j * 64 + u * 32, 32), 32)

    def unit_rows(j, u):
        return pl.ds(pl.multiple_of(j * 64 + u * 32, 32), 32)

    def stacked(j, part, q):
        cols = pl.ds(width * part + q * 256, 256)
        tcols = pl.ds(width * (part - 1) + q * 256, 256)
        both = []
        for u in range(2):
            t = jnp.concatenate([qkv[unit_rows(j, u), cols], tkv[text_rows(j, u), tcols]], axis=0)
            both.append(t)
        return jnp.concatenate(
            [jnp.concatenate([both[0], zero64], axis=1), jnp.concatenate([zero64, both[1]], axis=1)],
            axis=0,
        )

    def wide(ref, j, q):
        cols = pl.ds(q * 256, 256)
        return [head_blocks(ref[unit_rows(j, u), cols]) for u in range(2)]

    def gathered(full, u):
        parts = []
        for t in range(2):
            cols = slice(u * 256 + t * 128, u * 256 + t * 128 + 128)
            a = full[(2 * t) * 32 : (2 * t + 1) * 32, cols]
            b = full[(2 * t + 1) * 32 : (2 * t + 2) * 32, cols]
            parts.append(jnp.where(half32, a, b))
        return jnp.concatenate(parts, axis=1)

    def half_reduce(t, fill, op):
        a = op(jnp.where(left, t, fill), axis=1, keepdims=True)
        b = op(jnp.where(left, fill, t), axis=1, keepdims=True)
        return a, b

    def forward(j, carry):
        if negatives:
            n0 = lens[2 * j]
            n1 = lens[2 * j + 1]
            limit = jnp.where(uu == 0, n0, n1)
        else:
            n = [lens[4 * j + i] for i in range(4)]
            limit = jnp.where(
                uu == 0, jnp.where(qg == 0, n[0], n[1]), jnp.where(qg == 0, n[2], n[3])
            )
        valid32 = image_ok | (text_ok & (tpos < limit))
        valid32 = jnp.where(valid32, 1.0, 0.0)
        valid = jnp.concatenate([valid32] * 4, axis=0) > 0.5
        for q in range(quads):
            queries = wide(qkv, j, q)
            keys = stacked(j, 1, q)
            s = dot_nt(jnp.concatenate(queries, axis=1), keys) * scale
            s = jnp.where(valid, s, -1e30)
            m0, m1 = half_reduce(s, -3e38, jnp.max)
            e = jnp.exp(s - jnp.where(left, m0, m1))
            d0, d1 = half_reduce(e, 0.0, jnp.sum)
            p = e * jnp.where(left, 1.0 / d0, 1.0 / d1)
            probs[j, q] = p
            full = dot_nn(p.astype(BF), stacked(j, 2, q))
            for u in range(2):
                ctx[unit_rows(j, u), pl.ds(q * 256, 256)] = gathered(full, u).astype(BF)
        return carry

    lax.fori_loop(0, pairs_of_units, forward, 0)

    chunk = 128
    w0 = head_w[0:1, :]
    w1 = head_w[1:2, :]

    def middle(i, carry):
        rs = pl.ds(pl.multiple_of(i * chunk, chunk), chunk)
        hid = x[rs, :].astype(F32) + dot_nn(ctx[rs, :], wo[...])
        cen = hid - jnp.mean(hid, axis=1, keepdims=True)
        spread = jnp.mean(cen * cen, axis=1, keepdims=True)
        inv = lax.rsqrt(spread + 1e-06)
        xhat = cen * inv
        pooled = jnp.sum(xhat.reshape(chunk // 16, 16, width), axis=1) * (1.0 / 16.0)
        pooled = pooled * gain[...] + bias[...]
        l0 = jnp.sum(pooled * w0, axis=1, keepdims=True) + head_b[0]
        l1 = jnp.sum(pooled * w1, axis=1, keepdims=True) + head_b[1]
        cols = lax.broadcasted_iota(jnp.int32, (chunk // 16, 128), 1)
        logits[pl.ds(pl.multiple_of(i * (chunk // 16), chunk // 16), chunk // 16), :] = jnp.where(
            cols == 0, l0, l1
        )
        top = jnp.maximum(l0, l1)
        e0 = jnp.exp(l0 - top)
        e1 = jnp.exp(l1 - top)
        wrong = (e1 if negatives else e0) / (e0 + e1)
        slope = (w1 - w0) if negatives else (w0 - w1)
        dx = (wrong * (1.0 / 16.0)) * slope * gain[...]
        mean_dx = jnp.mean(dx, axis=1, keepdims=True)
        dx = jnp.broadcast_to(dx[:, None, :], (chunk // 16, 16, width)).reshape(chunk, width)
        mean_dx = jnp.broadcast_to(mean_dx[:, None, :], (chunk // 16, 16, 1)).reshape(chunk, 1)
        along = jnp.mean(dx * xhat, axis=1, keepdims=True)
        g = inv * (dx - mean_dx - xhat * along)
        gh[rs, :] = g
        gl = g.astype(BF)
        ga[rs, :] = gl
        dctx[rs, :] = dot_nt(gl, wo[...]).astype(BF)
        return carry

    lax.fori_loop(0, rows // chunk, middle, 0)

    def backward(j, carry):
        for q in range(quads):
            p = probs[j, q]
            dc = wide(dctx, j, q)
            dp = dot_nt(jnp.concatenate(dc, axis=1), stacked(j, 2, q))
            r0, r1 = half_reduce(dp * p, 0.0, jnp.sum)
            ds = (p * (dp - jnp.where(left, r0, r1)) * scale).astype(BF)
            full = dot_nn(ds, stacked(j, 1, q))
            for u in range(2):
                dqkv[unit_rows(j, u), pl.ds(q * 256, 256)] = gathered(full, u).astype(BF)
            queries = wide(qkv, j, q)
            dst = ds.T
            pt = p.astype(BF).T
            for part, lhs, rhs in ((1, dst, queries), (2, pt, dc)):
                outs = [dot_nn(lhs[u * 64 : u * 64 + 64], rhs[u]) for u in range(2)]
                for u in range(2):
                    dqkv[unit_rows(j, u), pl.ds(width * part + q * 256, 256)] = outs[u][:32].astype(BF)
                tcols = pl.ds(width * (part - 1) + q * 256, 256)
                if negatives:
                    tr = text_rows(j, 0)
                    total = text_in[tr, tcols] + outs[0][32:] + outs[1][32:]
                    dtext[tr, tcols] = total.astype(BF)
                else:
                    for u in range(2):
                        dtext[text_rows(j, u), tcols] = outs[u][32:]
        return carry

    lax.fori_loop(0, pairs_of_units, backward, 0)


def pair_core(negatives, lens, x, qkv, tkv, wo, gain, bias, head_w, head_b, text_in):
    rows, width = x.shape
    text_n = tkv.shape[0]
    body = functools.partial(core_kernel, negatives=negatives)
    if not negatives:
        def body(*refs):
            core_kernel(*refs[:9], None, *refs[9:], negatives=False)
    vm = pl.BlockSpec(memory_space=pltpu.VMEM)
    sm = pl.BlockSpec(memory_space=pltpu.SMEM)
    ins = [lens, x, qkv, tkv, wo, gain, bias, head_w, head_b]
    specs = [sm, vm, vm, vm, vm, vm, vm, vm, sm]
    if negatives:
        ins.append(text_in)
        specs.append(vm)
    out = [
        jax.ShapeDtypeStruct((rows // 16, 128), F32),
        jax.ShapeDtypeStruct((rows, width), F32),
        jax.ShapeDtypeStruct((rows, width), BF),
        jax.ShapeDtypeStruct((rows, width), BF),
        jax.ShapeDtypeStruct((rows, 3 * width), BF),
        jax.ShapeDtypeStruct((text_n, 2 * width), BF if negatives else F32),
    ]
    return pl.pallas_call(
        body,
        out_shape=out,
        in_specs=specs,
        out_specs=[vm] * len(out),
        scratch_shapes=[
            pltpu.VMEM((rows // 64, width // 256, 128, 128), F32),
            pltpu.VMEM((rows, width), BF),
        ],
        name="pair_core_neg" if negatives else "pair_core_pos",
        compiler_params=pltpu.CompilerParams(vmem_limit_bytes=48 * 1024 * 1024),
    )(*ins)


def grid_of(mesh):
    flat = list(mesh.devices.flat)
    sizes = [len({d.coords[a] for d in flat}) for a in range(3)]
    cores = len(flat) // (sizes[0] * sizes[1] * sizes[2])
    dims, stride = [], 1
    for s in [cores] + sizes:
        dims.append((stride, s))
        stride *= s
    return dims

def coord(dim):
    return (lax.axis_index("dp") // dim[0]) % dim[1]

def shifted(x, dim, k, n):
    stride, size = dim
    table = []
    for i in range(n):
        c = (i // stride) % size
        table.append((i, i + ((c + k) % size - c) * stride))
    return lax.ppermute(x, "dp", table)

def pick(x, dim, k):
    return lax.dynamic_index_in_dim(x, (coord(dim) + k) % dim[1], 0, keepdims=False)

def scatter_sum(x, dim, n):
    size = dim[1]
    if size == 1: return x
    parts = x.reshape((size, x.shape[0] // size) + x.shape[1:])
    got = [shifted(pick(parts, dim, k).astype(BF), dim, k, n) for k in range(1, size)]
    total = pick(parts, dim, 0).astype(F32)
    for g in got: total = total + g.astype(F32)
    return total.astype(BF)

def gather_rows(x, dim, n):
    size = dim[1]
    if size == 1: return x
    out = jnp.zeros((size,) + x.shape, x.dtype)
    out = lax.dynamic_update_index_in_dim(out, x, coord(dim), 0)
    for k in range(1, size):
        out = lax.dynamic_update_index_in_dim(out, shifted(x, dim, k, n), (coord(dim) - k) % size, 0)
    return out.reshape((size * x.shape[0],) + x.shape[1:])

def reduce_all(xs, orders, n):
    xs = list(xs)
    depth = len(orders[0])
    for s in range(depth):
        xs = [scatter_sum(x, o[s], n) for x, o in zip(xs, orders)]
    for s in reversed(range(depth)):
        xs = [gather_rows(x, o[s], n) for x, o in zip(xs, orders)]
    return xs


CAP = 2


def dot_tn(a, b):
    return lax.dot_general(a, b, (((0,), (0,)), ((), ())), preferred_element_type=F32)


def on_device(
    text_states,
    text_len,
    query_states,
    neg_owner,
    neg_slot,
    projection_weight,
    output_weight,
    ln_gain,
    ln_bias,
    itm_weight,
    itm_bias,
    *,
    dims,
):
    captions, text_rows, width = text_states.shape
    image_rows = query_states.shape[1]
    peers = lax.axis_size("dp")
    flat_owner = neg_owner.reshape(-1)
    flat_slot = neg_slot.reshape(-1)
    requests = flat_owner.shape[0]
    ids = jnp.arange(requests)
    same_owner = flat_owner[:, None] == flat_owner[None, :]
    before = ids[:, None] > ids[None, :]
    rank = jnp.sum((same_owner & before).astype(jnp.int32), axis=1)
    bucket = flat_owner * CAP + rank
    slot_hot = bucket[:, None] == jnp.arange(peers * CAP)[None, :]
    wanted = jnp.sum(jnp.where(slot_hot, flat_slot[:, None] + 1, 0), axis=0).reshape(peers, CAP)
    requested = lax.all_to_all(wanted, "dp", split_axis=0, concat_axis=0, tiled=True)
    send_select = (requested.reshape(-1)[:, None] == jnp.arange(captions)[None, :] + 1).astype(BF)
    outgoing = jnp.dot(send_select, query_states.reshape(captions, -1), preferred_element_type=F32)
    outgoing = outgoing.astype(BF).reshape(peers, CAP, image_rows, width)
    fetched = lax.all_to_all(outgoing, "dp", split_axis=0, concat_axis=0, tiled=True)
    take_select = slot_hot.astype(BF)

    text = text_states.reshape(captions * text_rows, width)
    own = query_states.reshape(captions * image_rows, width)
    gain = ln_gain[None]
    bias = ln_bias[None]
    head_w = itm_weight.T
    text_kv = dot_nn(text, projection_weight[:, width:]).astype(BF)
    own_qkv = dot_nn(own, projection_weight).astype(BF)
    own_logits, own_gh, own_ga, own_ctx, own_dqkv, own_dtext = pair_core(
        False, text_len, own, own_qkv, text_kv, output_weight, gain, bias, head_w, itm_bias, None
    )
    own_grad = dot_nt(own_dqkv, projection_weight) + own_gh

    negatives = jnp.dot(
        take_select, fetched.reshape(peers * CAP, -1), preferred_element_type=F32
    ).astype(BF)
    others = negatives.reshape(requests * image_rows, width)
    neg_qkv = dot_nn(others, projection_weight).astype(BF)
    neg_logits, neg_gh, neg_ga, neg_ctx, neg_dqkv, dtext = pair_core(
        True,
        text_len,
        others,
        neg_qkv,
        text_kv,
        output_weight,
        gain,
        bias,
        head_w,
        itm_bias,
        own_dtext,
    )
    neg_grad = (dot_nt(neg_dqkv, projection_weight) + neg_gh).astype(BF)
    outgoing_grads = jnp.dot(
        take_select.T, neg_grad.reshape(requests, -1), preferred_element_type=F32
    ).astype(BF)
    outgoing_grads = outgoing_grads.reshape(peers, CAP, image_rows, width)
    returned = lax.all_to_all(outgoing_grads, "dp", split_axis=0, concat_axis=0, tiled=True)

    d_out = dot_tn(own_ctx, own_ga) + dot_tn(neg_ctx, neg_ga)
    d_kv = dot_tn(text, dtext)
    d_qkv = dot_tn(own, own_dqkv) + dot_tn(others, neg_dqkv)
    grad_text = dot_nt(dtext, projection_weight[:, width:]).astype(BF)

    core_dim, x_dim, y_dim, z_dim = dims
    first = (core_dim, x_dim, y_dim, z_dim)
    second = (core_dim, y_dim, x_dim, z_dim)
    half = width + width // 2
    parts = [
        jnp.concatenate([d_qkv[:, :width], d_qkv[:, width : 2 * width] + d_kv[:, :width]], axis=1),
        jnp.concatenate([d_qkv[:, 2 * width :] + d_kv[:, width:], d_out], axis=1),
    ]
    summed = reduce_all(parts, [first, second], peers)
    summed = [s.astype(F32) * (1.0 / (captions * peers)) for s in summed]
    sum_qkv = jnp.concatenate([summed[0], summed[1][:, :width]], axis=1)
    sum_out = summed[1][:, width:]

    received = jnp.dot(
        send_select.T, returned.reshape(peers * CAP, -1), preferred_element_type=F32
    )
    grad_query = (
        own_grad.reshape(captions, image_rows, width)
        + received.reshape(captions, image_rows, width)
    ).astype(BF)
    logits = jnp.concatenate(
        [own_logits[:, None, :2], neg_logits[:, :2].reshape(captions, 2, 2)], axis=1
    )
    return (
        logits,
        grad_text.reshape(captions, text_rows, width),
        grad_query,
        sum_qkv,
        sum_out,
    )


def solution(mesh):
    dims = grid_of(mesh)
    placed = (
        P("dp", None, None),
        P("dp"),
        P("dp", None, None),
        P("dp", None),
        P("dp", None),
        P(),
        P(),
        P(),
        P(),
        P(),
        P(),
    )
    return jax.shard_map(
        functools.partial(on_device, dims=dims),
        mesh=mesh,
        in_specs=placed,
        out_specs=(P("dp", None, None), P("dp", None, None), P("dp", None, None), P(), P()),
        check_vma=False,
    )
```

time: 700 us -> 288 us (0.41); the launches traced: 691 us -> 286 us
  waiting for transfers between devices: 242 us -> 55.1 us
  matrix products: 179 us -> 44 us
  other arithmetic: 120 us -> 19.3 us
  Pallas kernels: 0 us -> 40.9 us
  local copies, waits for them, and re-layouts: 121 us -> 81.4 us
  starting transfers between devices: 13.8 us -> 44 us
  between operations: 15.2 us -> 1.73 us
    psum x1 -> x0, waiting for transfers between devices: 153 us -> none  [on_device(): lax.psum((projection_weight_gradient, output_weight_gradient), 'dp')]
    dot_general x21 -> x15, matrix products: 179 us -> 44 us  [the longest x5 16.1 us: dot_tn(): lax.dot_general(a, b, (((0,), (0,)), ((), ())), preferred_element_type=F32)]
    sub x2 -> x0, other arithmetic: 97.7 us -> none  [the longest x1 97.7 us: pair_work(): shifted = jnp.exp(scores - jnp.max(scores, axis=-1, keepdims=True))]
    all_to_all x1, waiting for transfers between devices: 49.5 us -> 0.01 us  [on_device(): lax.all_to_all(outgoing_grads, 'dp', split_axis=0, concat_axis=0, tiled=T...]
    ppermute x0 -> x24, waiting for transfers between devices: none -> 42.6 us  [shifted(): return lax.ppermute(x, 'dp', table)]
    pallas_call x0 -> x2, Pallas kernels: none -> 40.9 us  [pair_core(): pl.pallas_call(body, out_shape=out, in_specs=specs, out_specs=[vm] * len(...]
    reshape x9 -> x5, local copies, waits for them, and re-layouts: 53.3 us -> 17.2 us  [the longest x2 13.4 us: scatter_sum(): parts = x.reshape((size, x.shape[0] // size) + x.shape[1:])]
    transpose x3 -> x0, local copies, waits for them, and re-layouts: 32.9 us -> none  [matrix_product(): jnp.einsum(einsum_form, left_side, right_side, preferred_element_type=jnp...]
  transfers between devices with their start and end apart: 4 -> 27, of which waited for: 4 -> 11; matrix products, arithmetic and copies ran while one was open for 3% -> 38% of each run, Pallas kernels for 0% -> 5%
where the time goes in v1:
time: 288 us; the launch traced here: 286 us
  local copies, waits for them, and re-layouts  81.4 us (28%)
  waiting for transfers between devices  55.1 us (19%)
  starting transfers between devices  44 us (15%)
  matrix products  44 us (15%)
  Pallas kernels  40.9 us (14%)
  other arithmetic  19.3 us (7%)
    ppermute x24, waiting for transfers between devices, shifted(): return lax.ppermute(x, 'dp', table)  42.6 us
    pallas_call x2, Pallas kernels, pair_core(): pl.pallas_call(body, out_shape=out, in_specs=specs, out_specs=[vm] * len(...  40.9 us
    dynamic_slice x6, local copies, waits for them, and re-layouts, pick(): lax.dynamic_index_in_dim(x, (coord(dim) + k) % dim[1], 0, keepdims=False)  32.6 us
    ppermute x24, starting transfers between devices, shifted(): return lax.ppermute(x, 'dp', table)  29.4 us
    unnamed x70, local copies, waits for them, and re-layouts  24.1 us
    dot_general x5, matrix products, dot_tn(): lax.dot_general(a, b, (((0,), (0,)), ((), ())), preferred_element_type=F32)  16.1 us
    dot_general x3, matrix products, dot_nt(): lax.dot_general(a, b, (((1,), (1,)), ((), ())), preferred_element_type=F32)  13.5 us
    reshape x2, local copies, waits for them, and re-layouts, scatter_sum(): parts = x.reshape((size, x.shape[0] // size) + x.shape[1:])  13.4 us
  transfers between devices with their start and end apart: 27, of which 11 were waited for; matrix products, arithmetic and copies ran while one was open for 38% of the time, Pallas kernels for 5%

profile of v1, /device:TPU:0, one launch (start us, length us, event | category | flops | bytes accessed | tf_op | source)
XLA Modules:
  0.0 286.4 jit_solution(16568738785293199153)
XLA Ops:
  3.9 7.3 %all-to-all-start = ((s32[32,1,2]{2,1,0:T(1,128)}), s32[32,1,2]{2,1,0:T(1,128)S(1)}, u32[]{:S(2)}, u32[]{:S(2)}) async-start(s32[32,1,2]{2,1,0:T(1,128)} %bitcast.4), calls=%async_computation | async-start | bytes 32768 | tf_op jit(solution)/shard_map/all_to_all | solution.py:306
  12.4 6.0 %all-to-all-done = s32[32,1,2]{2,1,0:T(1,128)S(1)} async-done(((s32[32,1,2]{2,1,0:T(1,128)}), s32[32,1,2]{2,1,0:T(1,128)S(1)}, u32[]{:S(2)}, u32[]{:S(2)}) %all-to-all-start) | async-done | bytes 288 | tf_op jit(solution)/shard_map/all_to_all | solution.py:306
  21.8 3.6 %all-to-all-start.1 = ((bf16[32,2,16,768]{3,2,1,0:T(8,128)(2,1)}), bf16[32,2,16,768]{3,2,1,0:T(8,128)(2,1)}, u32[]{:S(2)}, u32[]{:S(2)}) async-start(bf16[32,2,16,768]{3,2,1,0:T(8,128)(2,1)} %bitcast.78), calls=%async_computation.1 | async-start | bytes 3145728 | tf_op jit(solution)/shard_map/all_to_all | solution.py:310
  29.7 14.0 %pair_core_pos.1 = (f32[16,128]{1,0:T(8,128)S(1)}, f32[256,768]{1,0:T(8,128)S(1)}, bf16[256,768]{1,0:T(8,128)(2,1)S(1)}, bf16[256,768]{1,0:T(8,128)(2,1)S(1)}, b...) custom-call(s32[16]{0:T(128)S(1)} %copy-done.9, bf16[256,768]{1,0:T(8,128)(2,1)S(1)} %bitcast.189, ...), custom_call_target="tpu_custom_call" | custom-call | tf_op jit(solution)/shard_map/pair_core_pos/pallas_call | solution.py:205
  48.4 4.0 %convolution_add_fusion.1 = f32[256,768]{1,0:T(8,128)} fusion(f32[256,768]{1,0:T(8,128)S(1)} %copy-done.14, bf16[256,2304]{1,0:T(8,128)(2,1)S(1)} %get-tuple-element.21, bf16[768,2304]{1,0:T(8,128)(2,1)} %param.16), kind=kOutput, calls=%fused_computation.28 | convolution fusion | flops 906166272 | bytes 6291456 | tf_op jit(solution)/shard_map/dot_general | solution.py:15
  52.5 4.1 %fusion.38 = f32[2304,768]{1,0:T(8,128)} fusion(bf16[256,2304]{1,0:T(8,128)(2,1)S(1)} %get-tuple-element.21, bf16[256,768]{1,0:T(8,128)(2,1)S(1)} %bitcast.190), kind=kOutput, calls=%fused_computation.102 | convolution fusion | flops 905969664 | bytes 8650752 | tf_op jit(solution)/shard_map/dot_general | solution.py:275
  56.6 6.6 %all-to-all-done.1 = bf16[32,2,16,768]{3,2,1,0:T(8,128)(2,1)} async-done(((bf16[32,2,16,768]{3,2,1,0:T(8,128)(2,1)}), bf16[32,2,16,768]{3,2,1,0:T(8,128)(2,1)}, u32[]{:S(2)}, u32[]{:S(2)}) %all-to-all-start.1) | async-done | bytes 1572896 | tf_op jit(solution)/shard_map/all_to_all | solution.py:310
  67.9 5.5 %convolution_convert_fusion.3.qkv = bf16[512,2304]{1,0:T(8,128)(2,1)} fusion(bf16[512,768]{1,0:T(8,128)(2,1)S(1)} %reshape.157.x, bf16[768,2304]{1,0:T(8,128)(2,1)} %param.16), kind=kOutput, calls=%fused_computation.9 | convolution fusion | flops 1813118976 | bytes 6684672 | tf_op jit(solution)/shard_map/dot_general | solution.py:19
  73.4 26.8 %pair_core_neg.1 = (f32[32,128]{1,0:T(8,128)S(1)}, f32[512,768]{1,0:T(8,128)}, bf16[512,768]{1,0:T(8,128)(2,1)S(1)}, bf16[512,768]{1,0:T(8,128)(2,1)S(1)}, bf16[...) custom-call(s32[16]{0:T(128)S(1)} %copy-done.10, bf16[512,768]{1,0:T(8,128)(2,1)S(1)} %reshape.157.x, ...), custom_call_target="tpu_custom_call" | custom-call | tf_op jit(solution)/shard_map/pair_core_neg/pallas_call | solution.py:205
  102.6 6.1 %add_convert_fusion = bf16[512,768]{1,0:T(8,128)(2,1)} fusion(f32[512,768]{1,0:T(8,128)} %get-tuple-element.24, bf16[512,2304]{1,0:T(8,128)(2,1)} %get-tuple-element.23, bf16[768,2304]{1,0:T(8,128)(2,1)} %param.16), kind=kOutput, calls=%fused_computation.26 | convolution fusion | flops 1812725760 | bytes 8257536 | tf_op jit(solution)/shard_map/dot_general | solution.py:15
  112.4 3.7 %all-to-all-start.2 = ((bf16[32,2,16,768]{3,2,1,0:T(8,128)(2,1)}), bf16[32,2,16,768]{3,2,1,0:T(8,128)(2,1)}, u32[]{:S(2)}, u32[]{:S(2)}) async-start(bf16[32,2,16,768]{3,2,1,0:T(8,128)(2,1)} %bitcast.197), calls=%async_computation.2 | async-start | bytes 3145728 | tf_op jit(solution)/shard_map/all_to_all | solution.py:348
  117.7 5.2 %bitcast_add_fusion = f32[768,2304]{0,1:T(8,128)S(1)} fusion(f32[2304,768]{1,0:T(8,128)} %fusion.38, bf16[512,768]{1,0:T(8,128)(2,1)S(1)} %reshape.157.x, bf16[512,2304]{1,0:T(8,128)(2,1)S(1)} %copy-done.19), kind=kOutput, calls=%fused_computation.4 | convolution fusion | flops 1813708800 | bytes 17301504 | tf_op jit(solution)/shard_map/dot_general | solution.py:275
  125.3 4.1 %convolution_add_fusion = f32[768,768]{0,1:T(8,128)} fusion(f32[768,768]{0,1:T(8,128)} %fusion.39, bf16[512,768]{1,0:T(8,128)(2,1)S(1)} %copy-done.5, bf16[512,768]{1,0:T(8,128)(2,1)S(1)} %get-tuple-element.28), kind=kOutput, calls=%fused_computation.22 | convolution fusion | flops 604569600 | bytes 6291456 | tf_op jit(solution)/shard_map/dot_general | solution.py:275
  129.3 6.0 %pad_maximum_fusion.1 = (f32[768,1536]{0,1:T(8,128)}, f32[768,1536]{0,1:T(8,128)}) fusion(f32[768,768]{0,1:T(8,128)S(1)} %get-tuple-element.53, f32[768,768]{0,1:T(8,128)S(1)} %copy-done.16, f32[768,768]{0,1:T(8,128)} %convolution_add_fusion, f32[768,768]{0,1:T(8,128)S(1)} %get-tuple-element.54), kind=kLoop, calls=%fused_computation.5 | loop fusion | flops 2359296 | bytes 18874368 | tf_op jit(solution)/shard_map/concatenate | solution.py:360
  135.3 6.7 %reshape.171 = f32[2,384,1536]{1,0,2:T(2,128)} reshape(f32[768,1536]{0,1:T(8,128)} %get-tuple-element.65) | data formatting | bytes 9437184 | tf_op jit(solution)/shard_map/reshape | solution.py:246
  142.0 5.3 %constant_dynamic-slice_fusion = bf16[1,384,1536]{1,0,2:T(2,128)(2,1)} fusion(f32[2,384,1536]{1,0,2:T(2,128)} %reshape.171, s32[]{:T(128)S(6)} %select_n.331), kind=kLoop, calls=%fused_computation.86 | loop fusion | bytes 2359300 | tf_op jit(solution)/shard_map/jit(dynamic_index_in_dim)/dynamic_slice | solution.py:241
  147.4 6.4 %copy.79 = bf16[1,384,1536]{2,1,0:T(8,128)(2,1)} copy(bf16[1,384,1536]{1,0,2:T(2,128)(2,1)} %constant_dynamic-slice_fusion) | data formatting | bytes 2359296
  154.0 6.7 %reshape.164 = f32[2,384,1536]{1,0,2:T(2,128)} reshape(f32[768,1536]{0,1:T(8,128)} %get-tuple-element.64) | data formatting | bytes 9437184 | tf_op jit(solution)/shard_map/reshape | solution.py:246
  160.7 5.3 %constant_dynamic-slice_fusion.2 = bf16[1,384,1536]{1,0,2:T(2,128)(2,1)} fusion(f32[2,384,1536]{1,0,2:T(2,128)} %reshape.164, s32[]{:T(128)S(6)} %select_n.331), kind=kLoop, calls=%fused_computation.88 | loop fusion | bytes 2359300 | tf_op jit(solution)/shard_map/jit(dynamic_index_in_dim)/dynamic_slice | solution.py:241
  166.0 5.5 %copy.78 = bf16[1,384,1536]{2,1,0:T(8,128)(2,1)S(1)} copy(bf16[1,384,1536]{1,0,2:T(2,128)(2,1)} %constant_dynamic-slice_fusion.2) | data formatting | bytes 2359296
  171.9 5.5 %constant_dynamic-slice_fusion.1 = f32[1,384,1536]{1,0,2:T(1,128)} fusion(f32[2,384,1536]{1,0,2:T(2,128)} %reshape.171, s32[]{:T(128)S(6)} %select_n.329), kind=kLoop, calls=%fused_computation.87 | loop fusion | bytes 4718596 | tf_op jit(solution)/shard_map/jit(dynamic_index_in_dim)/dynamic_slice | solution.py:241
  177.4 3.2 %constant_dynamic-slice_fusion.3 = f32[1,384,1536]{1,0,2:T(1,128)} fusion(f32[2,384,1536]{1,0,2:T(2,128)S(1)} %copy-done.15, s32[]{:T(128)S(6)} %select_n.329), kind=kLoop, calls=%fused_computation.89 | loop fusion | bytes 4718596 | tf_op jit(solution)/shard_map/jit(dynamic_index_in_dim)/dynamic_slice | solution.py:241
  181.1 6.6 %copy.72 = f32[1,384,1536]{2,1,0:T(8,128)} copy(f32[1,384,1536]{1,0,2:T(1,128)} %constant_dynamic-slice_fusion.1) | data formatting | bytes 4718592 | tf_op jit(solution)/shard_map/jit(dynamic_index_in_dim)/dynamic_slice | solution.py:241
  187.8 6.6 %copy.70 = f32[1,384,1536]{2,1,0:T(8,128)} copy(f32[1,384,1536]{1,0,2:T(1,128)} %constant_dynamic-slice_fusion.3) | data formatting | bytes 4718592 | tf_op jit(solution)/shard_map/jit(dynamic_index_in_dim)/dynamic_slice | solution.py:241
  194.4 3.4 %fusion.14 = bf16[256,768]{1,0:T(8,128)(2,1)} fusion(bf16[256,1536]{1,0:T(8,128)(2,1)S(1)} %get-tuple-element.20, bf16[768,2304]{1,0:T(8,128)(2,1)} %param.16), kind=kOutput, calls=%fused_computation.30 | convolution fusion | flops 604176384 | bytes 3538944 | tf_op jit(solution)/shard_map/dot_general | solution.py:15
  204.7 10.4 %collective-permute-done.13 = bf16[192,1536]{1,0:T(8,128)(2,1)S(1)} collective-permute-done((bf16[192,1536]{1,0:T(8,128)(2,1)S(1)}, bf16[192,1536]{1,0:T(8,128)(2,1)S(1)}, u32[]{:S(2)}, u32[]{:S(2)}) %collective-permute-start.13) | collective-permute-done | bytes 589856 | tf_op jit(solution)/shard_map/ppermute | solution.py:238
  219.6 5.0 %collective-permute-done.14 = bf16[96,1536]{1,0:T(8,128)(2,1)S(1)} collective-permute-done((bf16[96,1536]{1,0:T(8,128)(2,1)S(1)}, bf16[96,1536]{1,0:T(8,128)(2,1)S(1)}, u32[]{:S(2)}, u32[]{:S(2)}) %collective-permute-start.14) | collective-permute-done | bytes 294944 | tf_op jit(solution)/shard_map/ppermute | solution.py:238
  224.7 3.6 %collective-permute-start.17 = (bf16[24,1536]{1,0:T(8,128)(2,1)S(1)}, bf16[24,1536]{1,0:T(8,128)(2,1)S(1)}, u32[]{:S(2)}, u32[]{:S(2)}) collective-permute-start(bf16[24,1536]{1,0:T(8,128)(2,1)S(1)} %get-tuple-element.62), channel_id=1, source_target_pairs={{0,24},{1,25},{2,26},{3,27},{4,28},{5,29},{6,30},{7,31},{8,0},{9,1... | collective-permute-start | bytes 221192 | tf_op jit(solution)/shard_map/ppermute | solution.py:238
  233.5 4.1 %collective-permute-done.16 = bf16[24,1536]{1,0:T(8,128)(2,1)S(1)} collective-permute-done((bf16[24,1536]{1,0:T(8,128)(2,1)S(1)}, bf16[24,1536]{1,0:T(8,128)(2,1)S(1)}, u32[]{:S(2)}, u32[]{:S(2)}) %collective-permute-start.16) | collective-permute-done | bytes 73760 | tf_op jit(solution)/shard_map/ppermute | solution.py:238
  255.6 7.0 %collective-permute-done.9 = bf16[96,1536]{1,0:T(8,128)(2,1)S(1)} collective-permute-done((bf16[96,1536]{1,0:T(8,128)(2,1)S(1)}, bf16[96,1536]{1,0:T(8,128)(2,1)S(1)}, u32[]{:S(2)}, u32[]{:S(2)}) %collective-permute-start.9) | collective-permute-done | bytes 294944 | tf_op jit(solution)/shard_map/ppermute | solution.py:238
  264.4 9.2 %collective-permute-done.22 = bf16[192,1536]{1,0:T(8,128)(2,1)S(1)} collective-permute-done((bf16[192,1536]{1,0:T(8,128)(2,1)S(1)}, bf16[192,1536]{1,0:T(8,128)(2,1)S(1)}, u32[]{:S(2)}, u32[]{:S(2)}) %collective-permute-start.22) | collective-permute-done | bytes 589856 | tf_op jit(solution)/shard_map/ppermute | solution.py:238
  283.0 3.4 %pad_maximum_fusion = f32[768,2304]{1,0:T(8,128)} fusion(f32[768,768]{1,0:T(8,128)S(1)} %get-tuple-element.57, f32[768,1536]{1,0:T(8,128)S(1)} %bitcast.195), kind=kLoop, calls=%fused_computation.3 | loop fusion | flops 1769472 | bytes 14155776 | tf_op jit(solution)/shard_map/concatenate | solution.py:365
  (182 shorter events, 77.7 us)
Async XLA Ops:
  0.6 25.2 %copy-start = (bf16[16,16,768]{2,1,0:T(8,128)(2,1)S(1)}, bf16[16,16,768]{2,1,0:T(8,128)(2,1)}, u32[]{:S(2)}) copy-start(bf16[16,16,768]{2,1,0:T(8,128)(2,1)} %param.11) | copy-start | bytes 1179652
  3.9 14.4 %all-to-all-start = ((s32[32,1,2]{2,1,0:T(1,128)}), s32[32,1,2]{2,1,0:T(1,128)S(1)}, u32[]{:S(2)}, u32[]{:S(2)}) async-start(s32[32,1,2]{2,1,0:T(1,128)} %bitcast.4), calls=%async_computation | async-start | bytes 32768 | tf_op jit(solution)/shard_map/all_to_all | solution.py:306
  11.3 10.6 %copy-start.25 = (s32[16]{0:T(128)}, s32[16]{0:T(128)S(1)}, u32[]{:S(2)}) copy-start(s32[16]{0:T(128)S(1)} %iota_add_fusion) | copy-start | bytes 196
  21.8 41.3 %all-to-all-start.1 = ((bf16[32,2,16,768]{3,2,1,0:T(8,128)(2,1)}), bf16[32,2,16,768]{3,2,1,0:T(8,128)(2,1)}, u32[]{:S(2)}, u32[]{:S(2)}) async-start(bf16[32,2,16,768]{3,2,1,0:T(8,128)(2,1)} %bitcast.78), calls=%async_computation.1 | async-start | bytes 3145728 | tf_op jit(solution)/shard_map/all_to_all | solution.py:310
  56.6 8.5 %copy-start.28 = (s32[32]{0:T(128)S(1)}, s32[32]{0:T(128)}, u32[]{:S(2)}) copy-start(s32[32]{0:T(128)} %copy-done.27) | copy-start | bytes 388
  112.4 161.4 %all-to-all-start.2 = ((bf16[32,2,16,768]{3,2,1,0:T(8,128)(2,1)}), bf16[32,2,16,768]{3,2,1,0:T(8,128)(2,1)}, u32[]{:S(2)}, u32[]{:S(2)}) async-start(bf16[32,2,16,768]{3,2,1,0:T(8,128)(2,1)} %bitcast.197), calls=%async_computation.2 | async-start | bytes 3145728 | tf_op jit(solution)/shard_map/all_to_all | solution.py:348
  153.8 44.0 %collective-permute-start.12 = (bf16[384,1536]{1,0:T(8,128)(2,1)}, bf16[384,1536]{1,0:T(8,128)(2,1)}, u32[]{:S(2)}, u32[]{:S(2)}) collective-permute-start(bf16[384,1536]{1,0:T(8,128)(2,1)} %bitcast.147), channel_id=1, source_target_pairs={{0,1},{1,0},{2,3},{3,2},{4,5},{5,4},{6,7},{7,6},{8,9},{9,8},{10,11... | collective-permute-start | bytes 3538952 | tf_op jit(solution)/shard_map/ppermute | solution.py:238
  171.5 30.0 %collective-permute-start = (bf16[384,1536]{1,0:T(8,128)(2,1)S(1)}, bf16[384,1536]{1,0:T(8,128)(2,1)}, u32[]{:S(2)}, u32[]{:S(2)}) collective-permute-start(bf16[384,1536]{1,0:T(8,128)(2,1)S(1)} %bitcast.218), channel_id=1, source_target_pairs={{0,1},{1,0},{2,3},{3,2},{4,5},{5,4},{6,7},{7,6},{8,9},{9,8},{10,11... | collective-permute-start | bytes 3538952 | tf_op jit(solution)/shard_map/ppermute | solution.py:238
  199.7 15.4 %collective-permute-start.13 = (bf16[192,1536]{1,0:T(8,128)(2,1)S(1)}, bf16[192,1536]{1,0:T(8,128)(2,1)S(1)}, u32[]{:S(2)}, u32[]{:S(2)}) collective-permute-start(bf16[192,1536]{1,0:T(8,128)(2,1)S(1)} %dynamic-slice_bitcast_fusion), channel_id=1, source_target_pairs={{0,4},{1,5},{2,6},{3,7},{4,0},{5,1},{6,2},{7,3},{8,12},{9,13},{10,... | collective-permute-start | bytes 1769480 | tf_op jit(solution)/shard_map/ppermute | solution.py:238
  203.2 16.1 %collective-permute-start.1 = (bf16[192,1536]{1,0:T(8,128)(2,1)S(1)}, bf16[192,1536]{1,0:T(8,128)(2,1)S(1)}, u32[]{:S(2)}, u32[]{:S(2)}) collective-permute-start(bf16[192,1536]{1,0:T(8,128)(2,1)S(1)} %dynamic-slice_bitcast_fusion.1), channel_id=1, source_target_pairs={{0,2},{1,3},{2,0},{3,1},{4,6},{5,7},{6,4},{7,5},{8,10},{9,11},{10,... | collective-permute-start | bytes 1769480 | tf_op jit(solution)/shard_map/ppermute | solution.py:238
  215.3 9.3 %collective-permute-start.14 = (bf16[96,1536]{1,0:T(8,128)(2,1)S(1)}, bf16[96,1536]{1,0:T(8,128)(2,1)S(1)}, u32[]{:S(2)}, u32[]{:S(2)}) collective-permute-start(bf16[96,1536]{1,0:T(8,128)(2,1)S(1)} %dynamic-slice_bitcast_fusion.2), channel_id=1, source_target_pairs={{0,2},{1,3},{2,0},{3,1},{4,6},{5,7},{6,4},{7,5},{8,10},{9,11},{10,... | collective-permute-start | bytes 884744 | tf_op jit(solution)/shard_map/ppermute | solution.py:238
  219.5 9.9 %collective-permute-start.2 = (bf16[96,1536]{1,0:T(8,128)(2,1)S(1)}, bf16[96,1536]{1,0:T(8,128)(2,1)S(1)}, u32[]{:S(2)}, u32[]{:S(2)}) collective-permute-start(bf16[96,1536]{1,0:T(8,128)(2,1)S(1)} %dynamic-slice_bitcast_fusion.3), channel_id=1, source_target_pairs={{0,4},{1,5},{2,6},{3,7},{4,0},{5,1},{6,2},{7,3},{8,12},{9,13},{10,... | collective-permute-start | bytes 884744 | tf_op jit(solution)/shard_map/ppermute | solution.py:238
  224.7 8.8 %collective-permute-start.17 = (bf16[24,1536]{1,0:T(8,128)(2,1)S(1)}, bf16[24,1536]{1,0:T(8,128)(2,1)S(1)}, u32[]{:S(2)}, u32[]{:S(2)}) collective-permute-start(bf16[24,1536]{1,0:T(8,128)(2,1)S(1)} %get-tuple-element.62), channel_id=1, source_target_pairs={{0,24},{1,25},{2,26},{3,27},{4,28},{5,29},{6,30},{7,31},{8,0},{9,1... | collective-permute-start | bytes 221192 | tf_op jit(solution)/shard_map/ppermute | solution.py:238
  228.3 9.2 %collective-permute-start.16 = (bf16[24,1536]{1,0:T(8,128)(2,1)S(1)}, bf16[24,1536]{1,0:T(8,128)(2,1)S(1)}, u32[]{:S(2)}, u32[]{:S(2)}) collective-permute-start(bf16[24,1536]{1,0:T(8,128)(2,1)S(1)} %get-tuple-element.63), channel_id=1, source_target_pairs={{0,16},{1,17},{2,18},{3,19},{4,20},{5,21},{6,22},{7,23},{8,24},{9,... | collective-permute-start | bytes 221192 | tf_op jit(solution)/shard_map/ppermute | solution.py:238
  228.3 9.2 %collective-permute-start.15 = (bf16[24,1536]{1,0:T(8,128)(2,1)S(1)}, bf16[24,1536]{1,0:T(8,128)(2,1)S(1)}, u32[]{:S(2)}, u32[]{:S(2)}) collective-permute-start(bf16[24,1536]{1,0:T(8,128)(2,1)S(1)} %get-tuple-element.61), channel_id=1, source_target_pairs={{0,8},{1,9},{2,10},{3,11},{4,12},{5,13},{6,14},{7,15},{8,16},{9,17... | collective-permute-start | bytes 221192 | tf_op jit(solution)/shard_map/ppermute | solution.py:238
  229.5 11.2 %collective-permute-start.5 = (bf16[24,1536]{1,0:T(8,128)(2,1)S(1)}, bf16[24,1536]{1,0:T(8,128)(2,1)S(1)}, u32[]{:S(2)}, u32[]{:S(2)}) collective-permute-start(bf16[24,1536]{1,0:T(8,128)(2,1)S(1)} %get-tuple-element.59), channel_id=1, source_target_pairs={{0,24},{1,25},{2,26},{3,27},{4,28},{5,29},{6,30},{7,31},{8,0},{9,1... | collective-permute-start | bytes 221192 | tf_op jit(solution)/shard_map/ppermute | solution.py:238
  232.3 11.3 %collective-permute-start.4 = (bf16[24,1536]{1,0:T(8,128)(2,1)S(1)}, bf16[24,1536]{1,0:T(8,128)(2,1)S(1)}, u32[]{:S(2)}, u32[]{:S(2)}) collective-permute-start(bf16[24,1536]{1,0:T(8,128)(2,1)S(1)} %get-tuple-element.60), channel_id=1, source_target_pairs={{0,16},{1,17},{2,18},{3,19},{4,20},{5,21},{6,22},{7,23},{8,24},{9,... | collective-permute-start | bytes 221192 | tf_op jit(solution)/shard_map/ppermute | solution.py:238
  233.5 10.1 %collective-permute-start.3 = (bf16[24,1536]{1,0:T(8,128)(2,1)S(1)}, bf16[24,1536]{1,0:T(8,128)(2,1)S(1)}, u32[]{:S(2)}, u32[]{:S(2)}) collective-permute-start(bf16[24,1536]{1,0:T(8,128)(2,1)S(1)} %get-tuple-element.58), channel_id=1, source_target_pairs={{0,8},{1,9},{2,10},{3,11},{4,12},{5,13},{6,14},{7,15},{8,16},{9,17... | collective-permute-start | bytes 221192 | tf_op jit(solution)/shard_map/ppermute | solution.py:238
  237.6 7.8 %collective-permute-start.18 = (bf16[24,1536]{1,0:T(8,128)(2,1)S(1)}, bf16[24,1536]{1,0:T(8,128)(2,1)S(1)}, u32[]{:S(2)}, u32[]{:S(2)}) collective-permute-start(bf16[24,1536]{1,0:T(8,128)(2,1)S(1)} %get-tuple-element.52), channel_id=1, source_target_pairs={{0,8},{1,9},{2,10},{3,11},{4,12},{5,13},{6,14},{7,15},{8,16},{9,17... | collective-permute-start | bytes 221192 | tf_op jit(solution)/shard_map/ppermute | solution.py:238
  238.6 9.8 %collective-permute-start.19 = (bf16[24,1536]{1,0:T(8,128)(2,1)S(1)}, bf16[24,1536]{1,0:T(8,128)(2,1)S(1)}, u32[]{:S(2)}, u32[]{:S(2)}) collective-permute-start(bf16[24,1536]{1,0:T(8,128)(2,1)S(1)} %get-tuple-element.52), channel_id=1, source_target_pairs={{0,16},{1,17},{2,18},{3,19},{4,20},{5,21},{6,22},{7,23},{8,24},{9,... | collective-permute-start | bytes 221192 | tf_op jit(solution)/shard_map/ppermute | solution.py:238
  240.7 7.6 %collective-permute-start.20 = (bf16[24,1536]{1,0:T(8,128)(2,1)S(1)}, bf16[24,1536]{1,0:T(8,128)(2,1)S(1)}, u32[]{:S(2)}, u32[]{:S(2)}) collective-permute-start(bf16[24,1536]{1,0:T(8,128)(2,1)S(1)} %get-tuple-element.52), channel_id=1, source_target_pairs={{0,24},{1,25},{2,26},{3,27},{4,28},{5,29},{6,30},{7,31},{8,0},{9,1... | collective-permute-start | bytes 221192 | tf_op jit(solution)/shard_map/ppermute | solution.py:238
  243.7 6.6 %collective-permute-start.6 = (bf16[24,1536]{1,0:T(8,128)(2,1)S(1)}, bf16[24,1536]{1,0:T(8,128)(2,1)S(1)}, u32[]{:S(2)}, u32[]{:S(2)}) collective-permute-start(bf16[24,1536]{1,0:T(8,128)(2,1)S(1)} %get-tuple-element.50), channel_id=1, source_target_pairs={{0,8},{1,9},{2,10},{3,11},{4,12},{5,13},{6,14},{7,15},{8,16},{9,17... | collective-permute-start | bytes 221192 | tf_op jit(solution)/shard_map/ppermute | solution.py:238
  243.7 8.8 %collective-permute-start.7 = (bf16[24,1536]{1,0:T(8,128)(2,1)S(1)}, bf16[24,1536]{1,0:T(8,128)(2,1)S(1)}, u32[]{:S(2)}, u32[]{:S(2)}) collective-permute-start(bf16[24,1536]{1,0:T(8,128)(2,1)S(1)} %get-tuple-element.50), channel_id=1, source_target_pairs={{0,16},{1,17},{2,18},{3,19},{4,20},{5,21},{6,22},{7,23},{8,24},{9,... | collective-permute-start | bytes 221192 | tf_op jit(solution)/shard_map/ppermute | solution.py:238
  245.5 7.1 %collective-permute-start.8 = (bf16[24,1536]{1,0:T(8,128)(2,1)S(1)}, bf16[24,1536]{1,0:T(8,128)(2,1)S(1)}, u32[]{:S(2)}, u32[]{:S(2)}) collective-permute-start(bf16[24,1536]{1,0:T(8,128)(2,1)S(1)} %get-tuple-element.50), channel_id=1, source_target_pairs={{0,24},{1,25},{2,26},{3,27},{4,28},{5,29},{6,30},{7,31},{8,0},{9,1... | collective-permute-start | bytes 221192 | tf_op jit(solution)/shard_map/ppermute | solution.py:238
  248.4 6.8 %collective-permute-start.21 = (bf16[96,1536]{1,0:T(8,128)(2,1)S(1)}, bf16[96,1536]{1,0:T(8,128)(2,1)S(1)}, u32[]{:S(2)}, u32[]{:S(2)}) collective-permute-start(bf16[96,1536]{1,0:T(8,128)(2,1)S(1)} %bitcast.225), channel_id=1, source_target_pairs={{0,2},{1,3},{2,0},{3,1},{4,6},{5,7},{6,4},{7,5},{8,10},{9,11},{10,... | collective-permute-start | bytes 884744 | tf_op jit(solution)/shard_map/ppermute | solution.py:238
  252.6 9.9 %collective-permute-start.9 = (bf16[96,1536]{1,0:T(8,128)(2,1)S(1)}, bf16[96,1536]{1,0:T(8,128)(2,1)S(1)}, u32[]{:S(2)}, u32[]{:S(2)}) collective-permute-start(bf16[96,1536]{1,0:T(8,128)(2,1)S(1)} %bitcast.223), channel_id=1, source_target_pairs={{0,4},{1,5},{2,6},{3,7},{4,0},{5,1},{6,2},{7,3},{8,12},{9,13},{10,... | collective-permute-start | bytes 884744 | tf_op jit(solution)/shard_map/ppermute | solution.py:238
  255.2 18.4 %collective-permute-start.22 = (bf16[192,1536]{1,0:T(8,128)(2,1)S(1)}, bf16[192,1536]{1,0:T(8,128)(2,1)S(1)}, u32[]{:S(2)}, u32[]{:S(2)}) collective-permute-start(bf16[192,1536]{1,0:T(8,128)(2,1)S(1)} %bitcast.209), channel_id=1, source_target_pairs={{0,4},{1,5},{2,6},{3,7},{4,0},{5,1},{6,2},{7,3},{8,12},{9,13},{10,... | collective-permute-start | bytes 1769480 | tf_op jit(solution)/shard_map/ppermute | solution.py:238
  262.6 14.7 %collective-permute-start.10 = (bf16[192,1536]{1,0:T(8,128)(2,1)S(1)}, bf16[192,1536]{1,0:T(8,128)(2,1)S(1)}, u32[]{:S(2)}, u32[]{:S(2)}) collective-permute-start(bf16[192,1536]{1,0:T(8,128)(2,1)S(1)} %bitcast.211), channel_id=1, source_target_pairs={{0,2},{1,3},{2,0},{3,1},{4,6},{5,7},{6,4},{7,5},{8,10},{9,11},{10,... | collective-permute-start | bytes 1769480 | tf_op jit(solution)/shard_map/ppermute | solution.py:238
  264.2 9.6 %copy-start.21 = (s32[64]{0:T(128)S(1)}, s32[64]{0:T(128)}, u32[]{:S(2)}) copy-start(s32[64]{0:T(128)} %copy-done.20) | copy-start | bytes 772
  264.2 9.6 %copy-start.26 = (s32[16]{0:T(128)S(1)}, s32[16]{0:T(128)}, u32[]{:S(2)}) copy-start(s32[16]{0:T(128)} %copy-done.25) | copy-start | bytes 196
  273.7 4.7 %collective-permute-start.23 = (bf16[384,1536]{1,0:T(8,128)(2,1)S(1)}, bf16[384,1536]{1,0:T(8,128)(2,1)}, u32[]{:S(2)}, u32[]{:S(2)}) collective-permute-start(bf16[384,1536]{1,0:T(8,128)(2,1)S(1)} %bitcast.201), channel_id=1, source_target_pairs={{0,1},{1,0},{2,3},{3,2},{4,5},{5,4},{6,7},{7,6},{8,9},{9,8},{10,11... | collective-permute-start | bytes 3538952 | tf_op jit(solution)/shard_map/ppermute | solution.py:238
  277.3 4.9 %collective-permute-start.11 = (bf16[384,1536]{1,0:T(8,128)(2,1)S(1)}, bf16[384,1536]{1,0:T(8,128)(2,1)S(1)}, u32[]{:S(2)}, u32[]{:S(2)}) collective-permute-start(bf16[384,1536]{1,0:T(8,128)(2,1)S(1)} %bitcast.203), channel_id=1, source_target_pairs={{0,1},{1,0},{2,3},{3,2},{4,5},{5,4},{6,7},{7,6},{8,9},{9,8},{10,11... | collective-permute-start | bytes 3538952 | tf_op jit(solution)/shard_map/ppermute | solution.py:238
  (26 other events, 76.2 us)
